TPU v7x, 32 devices: a whole 2x2x4 slice. The times are simulated.
32 devices in a mesh: groups: 2 (over y), mem: 4 (over z), head: 2 (over x), width: 2 (over core).
Axes of the slice: x: 2, y: 2, z: 4, core: 2. Of those that a mesh axis runs over, the one named last changes fastest.
Arguments:
- residual_in: bfloat16 [64, 5120], P('groups', 'mem'), parts along dimension 0, may hold values from -26 to 26
- attention_gain: float32 [5120], P('mem'), may hold values from 0.5 to 1.5
- query_weight: bfloat16 [5120, 8192], P('mem', ('head', 'width')), may hold values from -0.078125 to 0.078125
- key_weight: bfloat16 [5120, 1024], P('mem', ('head', 'width')), may hold values from -0.078125 to 0.078125
- value_weight: bfloat16 [5120, 1024], P('mem', ('head', 'width')), may hold values from -0.078125 to 0.078125
- query_norm: float32 [128], replicated, may hold values from 0.25 to 1.75
- key_norm: float32 [128], replicated, may hold values from 0.1 to 1.9
- cache_keys: bfloat16 [65536, 8, 128], P(('groups', 'mem'), ('head', 'width')), parts along dimension 0, may hold values from -480 to 480
- cache_values: bfloat16 [65536, 8, 128], P(('groups', 'mem'), ('head', 'width')), parts along dimension 0, may hold values from -12 to 12
- slot_request: int32 [65536], P(('groups', 'mem')), parts along dimension 0, may hold values from 0 to 16, as said below
- lengths: int32 [32], P('groups'), parts along dimension 0, may hold values from 1056 to 1760, as said below
- output_weight: bfloat16 [8192, 5120], P(('head', 'width'), 'mem'), may hold values from -0.0625 to 0.0625
- second_gain: float32 [5120], P('mem'), may hold values from 0.5 to 1.5
- gate_weight: bfloat16 [5120, 25600], P('mem', ('head', 'width')), may hold values from -0.078125 to 0.078125
- up_weight: bfloat16 [5120, 25600], P('mem', ('head', 'width')), may hold values from -0.078125 to 0.078125
- down_weight: bfloat16 [25600, 5120], P(('head', 'width'), 'mem'), may hold values from -0.0390625 to 0.0390625
Outputs:
- layer_out: bfloat16 [64, 5120], P('groups', 'mem'), parts along dimension 0
There are 2 independent parts, one for each index of `groups`. A program takes and returns all parts, laid end to end along the dimension named above; an argument that names none is the same for every part. Nothing has to cross between parts.
Inputs may be any that keep to these rules, and one draw needn't show every extreme that they name: slot_request[s] names the request whose cached token sits in slot s, or is 16 for an empty slot. On each owner (each aligned block of 8192 slots along mem) the used slots come first; taking owners in order and their used slots in order, requests 0 to 15 follow one another in consecutive slots, so a request may continue on the next owner, but on no further one: a request's slots lie on at most two consecutive owners. Request r has exactly lengths[r] slots. Some owner has all its slots used. lengths[r] is the number of cached tokens of request r; its new tokens stand at positions lengths[r] and lengths[r] + 1.
All inputs are finite; a program needn't handle non-finite values.
Results may differ from a plain program's by a relative error of at most 0.0095.
The roundings to bfloat16 on the way count: a program that leaves them out, or rounds other values in their place, can miss the bound.
Values may be sent and summed in bfloat16 or wider, within the bound.
A program may use at most 128 MiB of HBM per device.

v0:
```python
import math
import jax
import jax.numpy as jnp
from jax import lax
from jax.sharding import PartitionSpec as P

D = 5120
epsilon = 1e-06
rope_base = 1000000.0
floor_score = -1e30


def combined_all(value, axis, join):
    pieces = jax.tree.map(lambda part: lax.all_gather(part, axis), value)
    head = jax.tree.map(lambda part: part[0], pieces)
    tail = jax.tree.map(lambda part: part[1:], pieces)
    running, _ = lax.scan(lambda running, slab: (join(running, slab), None), head, tail)
    return running


def rotate(values, places):
    breadth = values.shape[-1]
    halfway = breadth // 2
    frequency = rope_base ** (-(jnp.arange(halfway, dtype=jnp.float32) * 2.0) / breadth)
    angles = places[..., None] * frequency
    cosine = jnp.cos(angles)
    sine_part = jnp.sin(angles)
    leading = values[..., :halfway]
    trailing = values[..., halfway:]
    return jnp.concatenate(
        [leading * cosine - trailing * sine_part, trailing * cosine + leading * sine_part], axis=-1
    )


def head_norm(values, scaling):
    mean_square = jnp.mean(values * values, axis=-1, keepdims=True)
    return values * lax.rsqrt(mean_square + epsilon) * scaling


def combine(first, second):
    first_top, first_sum, first_acc = first
    second_top, second_sum, second_acc = second
    highest = jnp.maximum(first_top, second_top)
    first_factor = jnp.exp(first_top - highest)
    second_factor = jnp.exp(second_top - highest)
    return (
        highest,
        first_sum * first_factor + second_sum * second_factor,
        first_acc * first_factor[..., None] + second_acc * second_factor[..., None],
    )


def per_device(
    residual_in,
    attention_gain,
    query_weight,
    key_weight,
    value_weight,
    query_norm,
    key_norm,
    cache_keys,
    cache_values,
    slot_request,
    lengths,
    output_weight,
    second_gain,
    gate_weight,
    up_weight,
    down_weight,
):
    row_count = residual_in.shape[0]
    requests = row_count // 2
    head_dim = query_norm.shape[0]
    kv_here = cache_keys.shape[1]
    q_here = query_weight.shape[1] // head_dim
    group_size = q_here // kv_here
    score_scale = 1.0 / math.sqrt(head_dim)
    residual = residual_in.astype(jnp.float32)
    squares = lax.psum(jnp.sum(residual * residual, axis=1), "mem")
    normed = (residual * lax.rsqrt(squares / D + epsilon)[:, None] * attention_gain).astype(
        jnp.bfloat16
    )
    query_part = jnp.dot(normed, query_weight, preferred_element_type=jnp.float32)
    key_part = jnp.dot(normed, key_weight, preferred_element_type=jnp.float32)
    value_part = jnp.dot(normed, value_weight, preferred_element_type=jnp.float32)
    offsets = jnp.arange(2, dtype=jnp.int32)
    places = (lengths[:, None] + offsets[None, :]).reshape(row_count).astype(jnp.float32)
    query_sum, key_sum, value_sum = lax.psum((query_part, key_part, value_part), "mem")
    count_rows = query_sum.shape[0]
    query_rot = rotate(
        head_norm(query_sum.reshape(count_rows, q_here, head_dim), query_norm), places[:, None]
    )
    key_rot = rotate(
        head_norm(key_sum.reshape(count_rows, kv_here, head_dim), key_norm), places[:, None]
    )
    queries = query_rot.astype(jnp.bfloat16)
    new_keys = key_rot.astype(jnp.bfloat16)
    new_values = value_sum.reshape(count_rows, kv_here, head_dim).astype(jnp.bfloat16)
    queries_split = queries.reshape(row_count, kv_here, group_size, head_dim)
    row_owner = jnp.arange(row_count, dtype=jnp.int32) // 2
    capacity = cache_keys.shape[0]
    block_size = min(1024, capacity)
    used_slots = jnp.sum((slot_request < requests).astype(jnp.int32))
    used_blocks = (used_slots + block_size - 1) // block_size
    start_state = (
        jnp.full((row_count, kv_here, group_size), floor_score, jnp.float32),
        jnp.zeros((row_count, kv_here, group_size), jnp.float32),
        jnp.zeros((row_count, kv_here, group_size, head_dim), jnp.float32),
    )

    def visit_block(counter, carried):
        highest, summed, running = carried
        first_slot = counter * block_size
        key_block = lax.dynamic_slice_in_dim(cache_keys, first_slot, block_size, 0)
        value_block = lax.dynamic_slice_in_dim(cache_values, first_slot, block_size, 0)
        owner_block = lax.dynamic_slice_in_dim(slot_request, first_slot, block_size, 0)
        scores = (
            jnp.einsum(
                "bkgd,skd->bkgs", queries_split, key_block, preferred_element_type=jnp.float32
            )
            * score_scale
        )
        matches = (owner_block[None, :] == row_owner[:, None])[:, None, None, :]
        block_top = jnp.max(jnp.where(matches, scores, floor_score), axis=-1)
        updated = jnp.maximum(highest, block_top)
        weights = jnp.where(matches, jnp.exp(scores - updated[..., None]), 0.0)
        factor = jnp.exp(highest - updated)
        summed = summed * factor + jnp.sum(weights, axis=-1)
        running = running * factor[..., None] + jnp.einsum(
            "bkgs,skd->bkgd",
            weights.astype(jnp.bfloat16),
            value_block,
            preferred_element_type=jnp.float32,
        )
        return (updated, summed, running)

    highest, summed, running = lax.fori_loop(0, used_blocks, visit_block, start_state)
    highest, summed, running = combined_all((highest, summed, running), "mem", combine)
    query_pairs = queries.reshape(requests, 2, kv_here, group_size, head_dim)
    key_pairs = new_keys.reshape(requests, 2, kv_here, head_dim)
    value_pairs = new_values.reshape(requests, 2, kv_here, head_dim)
    allowed = (offsets[None, :] <= offsets[:, None])[None, :, None, None, :]
    allowed_rows = jnp.broadcast_to(allowed, (requests, 2, kv_here, group_size, 2)).reshape(
        row_count, kv_here, group_size, 2
    )
    own_scores = (
        jnp.einsum("rtkgd,rskd->rtkgs", query_pairs, key_pairs, preferred_element_type=jnp.float32)
        * score_scale
    )
    own_scores = jnp.where(allowed, own_scores, floor_score).reshape(
        row_count, kv_here, group_size, 2
    )
    final_top = jnp.maximum(highest, jnp.max(own_scores, axis=-1))
    own_weights = jnp.where(allowed_rows, jnp.exp(own_scores - final_top[..., None]), 0.0)
    factor = jnp.exp(highest - final_top)
    summed = summed * factor + jnp.sum(own_weights, axis=-1)
    own_rounded = own_weights.astype(jnp.bfloat16).reshape(requests, 2, kv_here, group_size, 2)
    own_values = jnp.einsum(
        "rtkgs,rskd->rtkgd", own_rounded, value_pairs, preferred_element_type=jnp.float32
    )
    running = running * factor[..., None] + own_values.reshape(
        row_count, kv_here, group_size, head_dim
    )
    attended = (
        (running / summed[..., None]).reshape(row_count, q_here * head_dim).astype(jnp.bfloat16)
    )
    projected = lax.psum(
        jnp.dot(attended, output_weight, preferred_element_type=jnp.float32), ("head", "width")
    )
    middle = (residual + projected).astype(jnp.bfloat16)
    middle_wide = middle.astype(jnp.float32)
    squares_mid = lax.psum(jnp.sum(middle_wide * middle_wide, axis=1), "mem")
    normed_mid = (middle_wide * lax.rsqrt(squares_mid / D + epsilon)[:, None] * second_gain).astype(
        jnp.bfloat16
    )
    gate_part = jnp.dot(normed_mid, gate_weight, preferred_element_type=jnp.float32)
    up_part = jnp.dot(normed_mid, up_weight, preferred_element_type=jnp.float32)
    gate_sum, up_sum = (
        lax.psum_scatter(gate_part, "mem", scatter_dimension=0, tiled=True),
        lax.psum_scatter(up_part, "mem", scatter_dimension=0, tiled=True),
    )
    activated = lax.all_gather(
        (jax.nn.silu(gate_sum) * up_sum).astype(jnp.bfloat16), "mem", axis=0, tiled=True
    )
    down_sum = lax.psum(
        jnp.dot(activated, down_weight, preferred_element_type=jnp.float32), ("head", "width")
    )
    return (middle_wide + down_sum).astype(jnp.bfloat16)


def solution(mesh):
    return jax.shard_map(
        per_device,
        mesh=mesh,
        in_specs=(
            P("groups", "mem"),
            P("mem"),
            P("mem", ("head", "width")),
            P("mem", ("head", "width")),
            P("mem", ("head", "width")),
            P(),
            P(),
            P(("groups", "mem"), ("head", "width"), None),
            P(("groups", "mem"), ("head", "width"), None),
            P(("groups", "mem")),
            P("groups"),
            P(("head", "width"), "mem"),
            P("mem"),
            P("mem", ("head", "width")),
            P("mem", ("head", "width")),
            P(("head", "width"), "mem"),
        ),
        out_specs=P("groups", "mem"),
        check_vma=False,
    )
```

profile of v0, /device:TPU:0, one launch (start us, length us, event | category | flops | bytes accessed | tf_op | source)
XLA Modules:
  0.0 318.0 jit_solution(10210930667824503828)
XLA Ops:
  6.6 1.1 fusion.24
  7.7 13.5 %psum.49 = f32[32]{0:T(128)S(1)} all-reduce(f32[32]{0:T(128)S(1)} %fusion.24), channel_id=1, replica_groups=mesh['groups'=2,'mem'=4,'head'=2,'width'=2] {'mem'}, use_global_device_ids=true, to_apply=%region_2.0 | all-reduce | flops 32 | bytes 256 | tf_op jit(solution)/shard_map/psum | solution.py:79
  21.1 3.6 %convolution_bitcast_fusion.1 = f32[4,8,16,128]{3,1,2,0:T(8,128)S(1)} fusion(bf16[1280,2048]{1,0:T(8,128)(2,1)} %param.22, bf16[32,1280]{1,0:T(8,128)(2,1)} %param.20, f32[1280]{0:T(1024)} %param.21, f32[32]{0:T(128)S(1)} %add_rsqrt_fusion.3), kind=kOutput, calls=%fused_computation.38 | convolution fusion | flops 167936000 | bytes 5592192 | tf_op jit(solution)/shard_map/dot_general | solution.py:83
  24.7 0.8 copy.134
  25.6 0.7 convert_reduce_fusion
  27.2 0.1 multiply_cosine_fusion
  27.3 32.1 %all-reduce.5.cloned.1.call-done = f32[32,16,128]{2,1,0:T(8,128)} async-done(((f32[32,16,128]{2,1,0:T(8,128)}), f32[32,16,128]{2,1,0:T(8,128)}) %all-reduce.5.cloned.1.call-update) | async-done | bytes 262160 | tf_op jit(solution)/shard_map/psum | solution.py:88
  59.5 1.1 multiply_reduce_fusion
  60.6 1.1 multiply_multiply_fusion
  61.7 0.2 subtract_convert_fusion
  62.0 0.1 pad_maximum_fusion
  62.2 12.0 %while.30 = (s32[]{:T(128)}, f32[32,2,8]{0,2,1:T(8,128)S(1)}, f32[32,2,8]{0,2,1:T(8,128)S(1)}, f32[32,2,8,128]{3,0,2,1:T(8,128)S(1)}, s32[]{:T(128)}, /*index=5*...) while((s32[]{:T(128)}, f32[32,2,8]{0,2,1:T(8,128)S(1)}, ...), condition=%wide.region_8.9_spmd.clone, body=%wide.region_5.8_spmd.clone.sunk | while | flops 274367744 | bytes 10269107 | solution.py:137
  62.2 0.1 broadcast_compare_fusion.2
  62.3 2.0 constant_dynamic-slice_fusion.6
  64.3 0.5 fusion.75
  64.9 0.6 fusion.76
  65.5 0.7 fusion.77
  66.3 0.1 broadcast_compare_fusion.2
  66.3 1.9 constant_dynamic-slice_fusion.6
  68.3 0.5 fusion.75
  68.8 0.6 fusion.76
  69.5 0.7 fusion.77
  70.2 0.1 broadcast_compare_fusion.2
  70.3 1.9 constant_dynamic-slice_fusion.6
  72.2 0.5 fusion.75
  72.8 0.6 fusion.76
  73.4 0.7 fusion.77
  74.2 0.7 copy-done.3
  75.0 0.2 convolution_bitcast_fusion.3
  75.3 0.2 fusion.45
  75.5 39.0 %all-reduce = (bf16[32,256]{1,0:T(8,128)(2,1)S(1)}, f32[32,2,128]{2,0,1:T(8,128)S(1)}) all-reduce(f32[32,256]{1,0:T(8,128)S(1)} %fusion.45, f32[32,2,128]{2,0,1:T(8,128)S(1)} %bitcast.129), channel_id=1, replica_groups=mesh['groups'=2,'mem'=4,'head'=2,'width'=2] {'mem'}, use_global_device_ids=true, to_apply=%region_14.15 | all-reduce | flops 16384 | bytes 114688 | tf_op jit(solution)/shard_map/psum | solution.py:88
  114.5 0.1 multiply_reduce_fusion.1
  114.7 0.1 subtract_convert_fusion.1
  114.9 14.1 %all-gather.1 = f32[128,2,8]{2,1,0:T(2,128)S(1)} all-gather(f32[32,2,8]{2,1,0:T(2,128)S(1)} %copy.92), channel_id=3, replica_groups=mesh['groups'=2,'mem'=4,'head'=2,'width'=2] {'mem'}, dimensions={0}, use_global_device_ids=true | all-gather | bytes 10240 | tf_op jit(solution)/shard_map/all_gather | solution.py:14
  129.0 0.1 copy.91
  129.0 13.3 %all-gather = f32[128,2,8]{2,1,0:T(2,128)S(1)} all-gather(f32[32,2,8]{2,1,0:T(2,128)S(1)} %copy.91), channel_id=2, replica_groups=mesh['groups'=2,'mem'=4,'head'=2,'width'=2] {'mem'}, dimensions={0}, use_global_device_ids=true | all-gather | bytes 10240 | tf_op jit(solution)/shard_map/all_gather | solution.py:14
  142.4 0.8 fusion.51
  143.5 0.1 copy.98
  143.6 1.0 slice.50
  144.6 0.2 copy.97
  144.8 1.2 slice.53
  146.0 1.7 while.29
  146.0 0.1 copy.174
  146.1 0.1 copy.175
  146.2 0.3 fusion.72
  146.8 0.3 fusion.72
  147.3 0.3 fusion.72
  147.7 0.2 fusion.43
  148.2 0.3 convolution_bitcast_fusion.2
  148.6 0.2 fusion.23
  148.8 4.1 %fusion.32 = f32[32,1280]{1,0:T(8,128)} fusion(bf16[2048,1280]{1,0:T(8,128)(2,1)} %param.31, bf16[4,8,16,128]{3,2,1,0:T(8,128)(2,1)S(1)} %bitcast.122), kind=kOutput, calls=%fused_computation.66 | convolution fusion | flops 167772160 | bytes 5537792 | tf_op jit(solution)/shard_map/dot_general | solution.py:168
  152.9 31.2 %all-reduce.7.cloned.1.call-done = f32[32,1280]{1,0:T(8,128)} async-done(((f32[32,1280]{1,0:T(8,128)}), f32[32,1280]{1,0:T(8,128)}) %all-reduce.7.cloned.1.call-update) | async-done | bytes 163856 | tf_op jit(solution)/shard_map/psum | solution.py:167
  184.1 1.0 fusion.28
  185.1 11.7 %psum.54 = f32[32]{0:T(128)S(1)} all-reduce(f32[32]{0:T(128)S(1)} %get-tuple-element.230), channel_id=1, replica_groups=mesh['groups'=2,'mem'=4,'head'=2,'width'=2] {'mem'}, use_global_device_ids=true, to_apply=%region_18.19 | all-reduce | flops 32 | bytes 256 | tf_op jit(solution)/shard_map/psum | solution.py:172
  196.8 9.6 %fusion.37 = f32[32,6400]{1,0:T(8,128)} fusion(bf16[1280,6400]{1,0:T(8,128)(2,1)} %param.34, bf16[32,1280]{1,0:T(8,128)(2,1)S(1)} %get-tuple-element.231, f32[1280]{0:T(1024)S(1)} %copy-done.5, f32[32]{0:T(128)S(1)} %add_rsqrt_fusion.2), kind=kOutput, calls=%fused_computation.82 | convolution fusion | flops 524451840 | bytes 17290368 | tf_op jit(solution)/shard_map/dot_general | solution.py:177
  206.4 0.2 reduce-scatter.3.cloned.1.call-start
  206.7 9.7 %fusion.39 = f32[32,6400]{1,0:T(8,128)} fusion(bf16[1280,6400]{1,0:T(8,128)(2,1)} %param.33, bf16[32,1280]{1,0:T(8,128)(2,1)S(1)} %get-tuple-element.231, f32[1280]{0:T(1024)S(1)} %copy-done.5, f32[32]{0:T(128)S(1)} %add_rsqrt_fusion.2), kind=kOutput, calls=%fused_computation.83 | convolution fusion | flops 524451840 | bytes 17290368 | tf_op jit(solution)/shard_map/dot_general | solution.py:176
  216.5 11.0 %reduce-scatter.5.cloned.1.call-done = f32[8,6400]{1,0:T(8,128)} async-done(((f32[32,6400]{1,0:T(8,128)}), f32[8,6400]{1,0:T(8,128)}) %reduce-scatter.5.cloned.1.call-update) | async-done | bytes 204816 | tf_op jit(solution)/shard_map/reduce_scatter | solution.py:180
  227.5 25.2 %reduce-scatter.3.cloned.1.call-done = f32[8,6400]{1,0:T(8,128)} async-done(((f32[32,6400]{1,0:T(8,128)}), f32[8,6400]{1,0:T(8,128)}) %reduce-scatter.3.cloned.1.call-update) | async-done | bytes 204816 | tf_op jit(solution)/shard_map/reduce_scatter | solution.py:179
  252.7 1.1 multiply_convert_fusion
  253.8 15.2 %all_gather.27 = bf16[32,6400]{1,0:T(8,128)(2,1)S(1)} all-gather(bf16[8,6400]{1,0:T(8,128)(2,1)S(1)} %multiply_convert_fusion), channel_id=1, replica_groups=mesh['groups'=2,'mem'=4,'head'=2,'width'=2] {'mem'}, dimensions={0}, use_global_device_ids=true | all-gather | bytes 512000 | tf_op jit(solution)/shard_map/all_gather | solution.py:182
  269.0 9.3 %fusion.52 = f32[32,1280]{1,0:T(8,128)} fusion(bf16[32,6400]{1,0:T(8,128)(2,1)S(1)} %all_gather.27, bf16[6400,1280]{1,0:T(8,128)(2,1)} %param.35), kind=kOutput, calls=%fused_computation.100 | convolution fusion | flops 524288000 | bytes 16957440 | tf_op jit(solution)/shard_map/dot_general | solution.py:186
  278.3 31.2 %all-reduce.9.cloned.1.call-done = f32[32,1280]{1,0:T(8,128)} async-done(((f32[32,1280]{1,0:T(8,128)}), f32[32,1280]{1,0:T(8,128)}) %all-reduce.9.cloned.1.call-update) | async-done | bytes 163856 | tf_op jit(solution)/shard_map/psum | solution.py:185
  309.5 1.6 fusion.31
  (92 shorter events, 2.1 us)
Async XLA Ops:
  6.5 68.4 %copy-start = (bf16[1280,256]{1,0:T(8,128)(2,1)S(1)}, bf16[1280,256]{1,0:T(8,128)(2,1)}, u32[]{:S(2)}) copy-start(bf16[1280,256]{1,0:T(8,128)(2,1)} %param.23) | copy-start | bytes 1966084
  6.5 19.0 %copy-start.6 = (s32[8192]{0:T(1024)S(1)}, s32[8192]{0:T(1024)}, u32[]{:S(2)}) copy-start(s32[8192]{0:T(1024)} %param.29) | copy-start | bytes 98308
  6.5 19.8 %copy-start.10 = (s32[16]{0:T(128)S(1)}, s32[16]{0:T(128)}, u32[]{:S(2)}) copy-start(s32[16]{0:T(128)} %param.30) | copy-start | bytes 196
  6.5 54.0 %copy-start.8 = (f32[128]{0:T(128)S(1)}, f32[128]{0:T(128)}, u32[]{:S(2)}) copy-start(f32[128]{0:T(128)} %param.25) | copy-start | bytes 1540
  6.5 52.9 %all-reduce.5.cloned.1.call-start = ((), (), s32[]{:S(2)}) async-start(), calls=%async_computation.2 | async-start | bytes 524288 | tf_op jit(solution)/shard_map/psum | solution.py:88
  25.5 118.1 %all-gather.5.cloned.1.call-start = ((), (), s32[]{:S(2)}) async-start(), calls=%async_computation.7 | async-start | bytes 1310720 | tf_op jit(solution)/shard_map/all_gather | solution.py:14
  62.1 12.8 %copy-start.2 = (bf16[32,1280]{1,0:T(8,128)(2,1)S(1)}, bf16[32,1280]{1,0:T(8,128)(2,1)}, u32[]{:S(2)}) copy-start(bf16[32,1280]{1,0:T(8,128)(2,1)} %param.20) | copy-start | bytes 245764
  62.1 12.8 %copy-start.7 = (f32[1280]{0:T(1024)S(1)}, f32[1280]{0:T(1024)}, u32[]{:S(2)}) copy-start(f32[1280]{0:T(1024)} %param.21) | copy-start | bytes 15364
  62.1 13.1 %copy-start.4 = (bf16[1280,256]{1,0:T(8,128)(2,1)S(1)}, bf16[1280,256]{1,0:T(8,128)(2,1)}, u32[]{:S(2)}) copy-start(bf16[1280,256]{1,0:T(8,128)(2,1)} %param.24) | copy-start | bytes 1966084
  62.2 52.4 %copy-start.9 = (f32[128]{0:T(128)S(1)}, f32[128]{0:T(128)}, u32[]{:S(2)}) copy-start(f32[128]{0:T(128)} %param.26) | copy-start | bytes 1540
  74.1 0.7 copy-start.3
  74.9 109.2 %all-reduce.7.cloned.1.call-start = ((), (), s32[]{:S(2)}) async-start(), calls=%async_computation.3 | async-start | bytes 327680 | tf_op jit(solution)/shard_map/psum | solution.py:167
  147.6 49.2 %copy-start.5 = (f32[1280]{0:T(1024)S(1)}, f32[1280]{0:T(1024)}, u32[]{:S(2)}) copy-start(f32[1280]{0:T(1024)} %param.32) | copy-start | bytes 15364
  152.9 74.6 %reduce-scatter.5.cloned.1.call-start = ((), (), s32[]{:S(2)}) async-start(), calls=%async_computation.5 | async-start | bytes 1024000 | tf_op jit(solution)/shard_map/reduce_scatter | solution.py:180
  206.4 46.3 %reduce-scatter.3.cloned.1.call-start = ((), (), s32[]{:S(2)}) async-start(), calls=%async_computation.4 | async-start | bytes 1024000 | tf_op jit(solution)/shard_map/reduce_scatter | solution.py:179
  216.4 93.1 %all-reduce.9.cloned.1.call-start = ((), (), s32[]{:S(2)}) async-start(), calls=%async_computation.6 | async-start | bytes 327680 | tf_op jit(solution)/shard_map/psum | solution.py:185
  269.0 42.1 %copy-start.1 = (bf16[1280,256]{1,0:T(8,128)(2,1)S(1)}, bf16[1280,256]{1,0:T(8,128)(2,1)}, u32[]{:S(2)}) copy-start(bf16[1280,256]{1,0:T(8,128)(2,1)} %param.23) | copy-start | bytes 1966084
Sparse Core Ops, SparseCore 0:
  25.6 33.7 all-reduce.4
  75.0 50.2 all-gather.4
  153.0 31.0 all-reduce.6
  206.6 20.8 reduce-scatter.4
  229.6 22.9 reduce-scatter.2
  278.4 31.0 all-reduce.8
where the time goes:
time: 319 us; the launch traced here: 318 us
  waiting for transfers between devices  131 us (41%)
  blocking collectives  107 us (34%)
  matrix products  41.5 us (13%)
  between operations  14.6 us (5%)
  other arithmetic  12 us (4%)
  local copies, waits for them, and re-layouts  11.5 us (4%)
    psum x1, blocking collectives, per_device(): lax.psum((query_part, key_part, value_part), 'mem')  39 us
    psum x1, waiting for transfers between devices, per_device(): lax.psum((query_part, key_part, value_part), 'mem')  32.1 us
    psum x1, waiting for transfers between devices, per_device(): lax.psum(jnp.dot(activated, down_weight, preferred_element_type=jnp.float...  31.2 us
    psum x1, waiting for transfers between devices, per_device(): lax.psum(jnp.dot(attended, output_weight, preferred_element_type=jnp.floa...  31.2 us
    all_gather x2, blocking collectives, combined_all(): pieces = jax.tree.map(lambda part: lax.all_gather(part, axis), value)  27.4 us
    reduce_scatter x1, waiting for transfers between devices, per_device(): lax.psum_scatter(gate_part, 'mem', scatter_dimension=0, tiled=True)  25.2 us
    all_gather x1, blocking collectives, per_device(): lax.all_gather((jax.nn.silu(gate_sum) * up_sum).astype(jnp.bfloat16), 'me...  15.2 us
    psum x1, blocking collectives, per_device(): squares = lax.psum(jnp.sum(residual * residual, axis=1), 'mem')  13.5 us
  transfers between devices with their start and end apart: 6, of which 5 were waited for; matrix products, arithmetic and copies ran while one was open for 4% of the time, Pallas kernels for 0%

commit v1 on v0

--- a/solution.py
+++ b/solution.py
@@ -183,7 +183,8 @@
         (jax.nn.silu(gate_sum) * up_sum).astype(jnp.bfloat16), "mem", axis=0, tiled=True
     )
     down_sum = lax.psum(
-        jnp.dot(activated, down_weight, preferred_element_type=jnp.float32), ("head", "width")
+        lax.psum(jnp.dot(activated, down_weight, preferred_element_type=jnp.float32), "width"),
+        "head",
     )
     return (middle_wide + down_sum).astype(jnp.bfloat16)
 

time: 319 us -> 330 us (1.034)
  waiting for transfers between devices: 131 us -> 142 us
    psum x0 -> x1, waiting for transfers between devices: none -> 25.5 us  [per_device(): lax.psum(lax.psum(jnp.dot(activated, down_weight, preferred_element_type=...]
    psum x1, waiting for transfers between devices: 31.2 us -> 17.3 us  [per_device(): lax.psum(jnp.dot(activated, down_weight, preferred_element_type=jnp.float...]
  transfers between devices with their start and end apart: 6 -> 7, of which waited for: 5 -> 6; matrix products, arithmetic and copies ran while one was open for 4% -> 4% of each run, Pallas kernels for 0% -> 0%
where the time goes in v1:
time: 330 us
  waiting for transfers between devices  142 us (43%)
  blocking collectives  107 us (32%)
  matrix products  41.5 us (13%)
  between operations  14.6 us (4%)
  other arithmetic  12 us (4%)
  local copies, waits for them, and re-layouts  11.5 us (3%)
    psum x1, blocking collectives, per_device(): lax.psum((query_part, key_part, value_part), 'mem')  39 us
    psum x1, waiting for transfers between devices, per_device(): lax.psum((query_part, key_part, value_part), 'mem')  32.1 us
    psum x1, waiting for transfers between devices, per_device(): lax.psum(jnp.dot(attended, output_weight, preferred_element_type=jnp.floa...  31.2 us
    all_gather x2, blocking collectives, combined_all(): pieces = jax.tree.map(lambda part: lax.all_gather(part, axis), value)  27.4 us
    psum x1, waiting for transfers between devices, per_device(): lax.psum(lax.psum(jnp.dot(activated, down_weight, preferred_element_type=...  25.5 us
    reduce_scatter x1, waiting for transfers between devices, per_device(): lax.psum_scatter(gate_part, 'mem', scatter_dimension=0, tiled=True)  25.2 us
    psum x1, waiting for transfers between devices, per_device(): lax.psum(jnp.dot(activated, down_weight, preferred_element_type=jnp.float...  17.3 us
    all_gather x1, blocking collectives, per_device(): lax.all_gather((jax.nn.silu(gate_sum) * up_sum).astype(jnp.bfloat16), 'me...  15.2 us
  transfers between devices with their start and end apart: 7, of which 6 were waited for; matrix products, arithmetic and copies ran while one was open for 4% of the time, Pallas kernels for 0%

profile of v1, /device:TPU:0, one launch (start us, length us, event | category | flops | bytes accessed | tf_op | source)
XLA Modules:
  0.0 329.5 jit_solution(17447321221726007010)
XLA Ops:
  6.6 1.1 fusion.24
  7.7 13.5 %psum.56 = f32[32]{0:T(128)S(1)} all-reduce(f32[32]{0:T(128)S(1)} %fusion.24), channel_id=1, replica_groups=mesh['groups'=2,'mem'=4,'head'=2,'width'=2] {'mem'}, use_global_device_ids=true, to_apply=%region_2.0 | all-reduce | flops 32 | bytes 256 | tf_op jit(solution)/shard_map/psum | solution.py:79
  21.1 3.6 %convolution_bitcast_fusion.1 = f32[4,8,16,128]{3,1,2,0:T(8,128)S(1)} fusion(bf16[1280,2048]{1,0:T(8,128)(2,1)} %param.22, bf16[32,1280]{1,0:T(8,128)(2,1)} %param.20, f32[1280]{0:T(1024)} %param.21, f32[32]{0:T(128)S(1)} %add_rsqrt_fusion.3), kind=kOutput, calls=%fused_computation.38 | convolution fusion | flops 167936000 | bytes 5592192 | tf_op jit(solution)/shard_map/dot_general | solution.py:83
  24.7 0.8 copy.134
  25.6 0.7 convert_reduce_fusion
  27.2 0.1 multiply_cosine_fusion
  27.3 32.1 %all-reduce.6.cloned.1.call-done = f32[32,16,128]{2,1,0:T(8,128)} async-done(((f32[32,16,128]{2,1,0:T(8,128)}), f32[32,16,128]{2,1,0:T(8,128)}) %all-reduce.6.cloned.1.call-update) | async-done | bytes 262160 | tf_op jit(solution)/shard_map/psum | solution.py:88
  59.5 1.1 multiply_reduce_fusion
  60.6 1.1 multiply_multiply_fusion
  61.7 0.2 subtract_convert_fusion
  62.0 0.1 pad_maximum_fusion
  62.2 12.0 %while.30 = (s32[]{:T(128)}, f32[32,2,8]{0,2,1:T(8,128)S(1)}, f32[32,2,8]{0,2,1:T(8,128)S(1)}, f32[32,2,8,128]{3,0,2,1:T(8,128)S(1)}, s32[]{:T(128)}, /*index=5*...) while((s32[]{:T(128)}, f32[32,2,8]{0,2,1:T(8,128)S(1)}, ...), condition=%wide.region_8.9_spmd.clone, body=%wide.region_5.8_spmd.clone.sunk | while | flops 274367744 | bytes 10269107 | solution.py:137
  62.2 0.1 broadcast_compare_fusion.2
  62.3 2.0 constant_dynamic-slice_fusion.6
  64.3 0.5 fusion.75
  64.9 0.6 fusion.76
  65.5 0.7 fusion.77
  66.3 0.1 broadcast_compare_fusion.2
  66.3 1.9 constant_dynamic-slice_fusion.6
  68.3 0.5 fusion.75
  68.8 0.6 fusion.76
  69.5 0.7 fusion.77
  70.2 0.1 broadcast_compare_fusion.2
  70.3 1.9 constant_dynamic-slice_fusion.6
  72.2 0.5 fusion.75
  72.8 0.6 fusion.76
  73.4 0.7 fusion.77
  74.2 0.7 copy-done.3
  75.0 0.2 convolution_bitcast_fusion.3
  75.3 0.2 fusion.45
  75.5 39.0 %all-reduce = (bf16[32,256]{1,0:T(8,128)(2,1)S(1)}, f32[32,2,128]{2,0,1:T(8,128)S(1)}) all-reduce(f32[32,256]{1,0:T(8,128)S(1)} %fusion.45, f32[32,2,128]{2,0,1:T(8,128)S(1)} %bitcast.129), channel_id=1, replica_groups=mesh['groups'=2,'mem'=4,'head'=2,'width'=2] {'mem'}, use_global_device_ids=true, to_apply=%region_14.15 | all-reduce | flops 16384 | bytes 114688 | tf_op jit(solution)/shard_map/psum | solution.py:88
  114.5 0.1 multiply_reduce_fusion.1
  114.7 0.1 subtract_convert_fusion.1
  114.9 14.1 %all-gather.1 = f32[128,2,8]{2,1,0:T(2,128)S(1)} all-gather(f32[32,2,8]{2,1,0:T(2,128)S(1)} %copy.92), channel_id=3, replica_groups=mesh['groups'=2,'mem'=4,'head'=2,'width'=2] {'mem'}, dimensions={0}, use_global_device_ids=true | all-gather | bytes 10240 | tf_op jit(solution)/shard_map/all_gather | solution.py:14
  129.0 0.1 copy.91
  129.0 13.3 %all-gather = f32[128,2,8]{2,1,0:T(2,128)S(1)} all-gather(f32[32,2,8]{2,1,0:T(2,128)S(1)} %copy.91), channel_id=2, replica_groups=mesh['groups'=2,'mem'=4,'head'=2,'width'=2] {'mem'}, dimensions={0}, use_global_device_ids=true | all-gather | bytes 10240 | tf_op jit(solution)/shard_map/all_gather | solution.py:14
  142.4 0.8 fusion.51
  143.5 0.1 copy.98
  143.6 1.0 slice.50
  144.6 0.2 copy.97
  144.8 1.2 slice.53
  146.0 1.7 while.29
  146.0 0.1 copy.174
  146.2 0.3 fusion.72
  146.8 0.3 fusion.72
  147.3 0.3 fusion.72
  147.7 0.2 fusion.43
  148.2 0.3 convolution_bitcast_fusion.2
  148.6 0.2 fusion.23
  148.8 4.1 %fusion.32 = f32[32,1280]{1,0:T(8,128)} fusion(bf16[2048,1280]{1,0:T(8,128)(2,1)} %param.31, bf16[4,8,16,128]{3,2,1,0:T(8,128)(2,1)S(1)} %bitcast.122), kind=kOutput, calls=%fused_computation.66 | convolution fusion | flops 167772160 | bytes 5537792 | tf_op jit(solution)/shard_map/dot_general | solution.py:168
  152.9 31.2 %all-reduce.8.cloned.1.call-done = f32[32,1280]{1,0:T(8,128)} async-done(((f32[32,1280]{1,0:T(8,128)}), f32[32,1280]{1,0:T(8,128)}) %all-reduce.8.cloned.1.call-update) | async-done | bytes 163856 | tf_op jit(solution)/shard_map/psum | solution.py:167
  184.1 1.0 fusion.28
  185.1 11.7 %psum.61 = f32[32]{0:T(128)S(1)} all-reduce(f32[32]{0:T(128)S(1)} %get-tuple-element.230), channel_id=1, replica_groups=mesh['groups'=2,'mem'=4,'head'=2,'width'=2] {'mem'}, use_global_device_ids=true, to_apply=%region_18.19 | all-reduce | flops 32 | bytes 256 | tf_op jit(solution)/shard_map/psum | solution.py:172
  196.8 9.6 %fusion.37 = f32[32,6400]{1,0:T(8,128)} fusion(bf16[1280,6400]{1,0:T(8,128)(2,1)} %param.34, bf16[32,1280]{1,0:T(8,128)(2,1)S(1)} %get-tuple-element.231, f32[1280]{0:T(1024)S(1)} %copy-done.5, f32[32]{0:T(128)S(1)} %add_rsqrt_fusion.2), kind=kOutput, calls=%fused_computation.82 | convolution fusion | flops 524451840 | bytes 17290368 | tf_op jit(solution)/shard_map/dot_general | solution.py:177
  206.4 0.2 reduce-scatter.3.cloned.1.call-start
  206.7 9.7 %fusion.39 = f32[32,6400]{1,0:T(8,128)} fusion(bf16[1280,6400]{1,0:T(8,128)(2,1)} %param.33, bf16[32,1280]{1,0:T(8,128)(2,1)S(1)} %get-tuple-element.231, f32[1280]{0:T(1024)S(1)} %copy-done.5, f32[32]{0:T(128)S(1)} %add_rsqrt_fusion.2), kind=kOutput, calls=%fused_computation.83 | convolution fusion | flops 524451840 | bytes 17290368 | tf_op jit(solution)/shard_map/dot_general | solution.py:176
  216.5 11.0 %reduce-scatter.5.cloned.1.call-done = f32[8,6400]{1,0:T(8,128)} async-done(((f32[32,6400]{1,0:T(8,128)}), f32[8,6400]{1,0:T(8,128)}) %reduce-scatter.5.cloned.1.call-update) | async-done | bytes 204816 | tf_op jit(solution)/shard_map/reduce_scatter | solution.py:180
  227.5 25.2 %reduce-scatter.3.cloned.1.call-done = f32[8,6400]{1,0:T(8,128)} async-done(((f32[32,6400]{1,0:T(8,128)}), f32[8,6400]{1,0:T(8,128)}) %reduce-scatter.3.cloned.1.call-update) | async-done | bytes 204816 | tf_op jit(solution)/shard_map/reduce_scatter | solution.py:179
  252.7 1.1 multiply_convert_fusion
  253.8 15.2 %all_gather.27 = bf16[32,6400]{1,0:T(8,128)(2,1)S(1)} all-gather(bf16[8,6400]{1,0:T(8,128)(2,1)S(1)} %multiply_convert_fusion), channel_id=1, replica_groups=mesh['groups'=2,'mem'=4,'head'=2,'width'=2] {'mem'}, dimensions={0}, use_global_device_ids=true | all-gather | bytes 512000 | tf_op jit(solution)/shard_map/all_gather | solution.py:182
  269.0 9.3 %fusion.52 = f32[32,1280]{1,0:T(8,128)} fusion(bf16[32,6400]{1,0:T(8,128)(2,1)S(1)} %all_gather.27, bf16[6400,1280]{1,0:T(8,128)(2,1)} %param.35), kind=kOutput, calls=%fused_computation.100 | convolution fusion | flops 524288000 | bytes 16957440 | tf_op jit(solution)/shard_map/dot_general | solution.py:186
  278.4 17.3 %all-reduce.10.cloned.1.call-done = f32[32,1280]{1,0:T(8,128)} async-done(((f32[32,1280]{1,0:T(8,128)}), f32[32,1280]{1,0:T(8,128)}) %all-reduce.10.cloned.1.call-update) | async-done | bytes 163856 | tf_op jit(solution)/shard_map/psum | solution.py:186
  295.7 25.5 %all-reduce.12.cloned.1.call-done = f32[32,1280]{1,0:T(8,128)} async-done(((f32[32,1280]{1,0:T(8,128)}), f32[32,1280]{1,0:T(8,128)}) %all-reduce.12.cloned.1.call-update) | async-done | bytes 163856 | tf_op jit(solution)/shard_map/psum | solution.py:185
  321.1 1.6 fusion.31
  (95 shorter events, 2.3 us)
Async XLA Ops:
  6.5 68.4 %copy-start = (bf16[1280,256]{1,0:T(8,128)(2,1)S(1)}, bf16[1280,256]{1,0:T(8,128)(2,1)}, u32[]{:S(2)}) copy-start(bf16[1280,256]{1,0:T(8,128)(2,1)} %param.23) | copy-start | bytes 1966084
  6.5 19.0 %copy-start.6 = (s32[8192]{0:T(1024)S(1)}, s32[8192]{0:T(1024)}, u32[]{:S(2)}) copy-start(s32[8192]{0:T(1024)} %param.29) | copy-start | bytes 98308
  6.5 19.8 %copy-start.10 = (s32[16]{0:T(128)S(1)}, s32[16]{0:T(128)}, u32[]{:S(2)}) copy-start(s32[16]{0:T(128)} %param.30) | copy-start | bytes 196
  6.5 54.0 %copy-start.8 = (f32[128]{0:T(128)S(1)}, f32[128]{0:T(128)}, u32[]{:S(2)}) copy-start(f32[128]{0:T(128)} %param.25) | copy-start | bytes 1540
  6.5 52.9 %all-reduce.6.cloned.1.call-start = ((), (), s32[]{:S(2)}) async-start(), calls=%async_computation.2 | async-start | bytes 524288 | tf_op jit(solution)/shard_map/psum | solution.py:88
  25.5 118.1 %all-gather.5.cloned.1.call-start = ((), (), s32[]{:S(2)}) async-start(), calls=%async_computation.8 | async-start | bytes 1310720 | tf_op jit(solution)/shard_map/all_gather | solution.py:14
  62.1 12.8 %copy-start.2 = (bf16[32,1280]{1,0:T(8,128)(2,1)S(1)}, bf16[32,1280]{1,0:T(8,128)(2,1)}, u32[]{:S(2)}) copy-start(bf16[32,1280]{1,0:T(8,128)(2,1)} %param.20) | copy-start | bytes 245764
  62.1 12.8 %copy-start.7 = (f32[1280]{0:T(1024)S(1)}, f32[1280]{0:T(1024)}, u32[]{:S(2)}) copy-start(f32[1280]{0:T(1024)} %param.21) | copy-start | bytes 15364
  62.1 13.1 %copy-start.4 = (bf16[1280,256]{1,0:T(8,128)(2,1)S(1)}, bf16[1280,256]{1,0:T(8,128)(2,1)}, u32[]{:S(2)}) copy-start(bf16[1280,256]{1,0:T(8,128)(2,1)} %param.24) | copy-start | bytes 1966084
  62.2 52.4 %copy-start.9 = (f32[128]{0:T(128)S(1)}, f32[128]{0:T(128)}, u32[]{:S(2)}) copy-start(f32[128]{0:T(128)} %param.26) | copy-start | bytes 1540
  74.1 0.7 copy-start.3
  74.9 109.2 %all-reduce.8.cloned.1.call-start = ((), (), s32[]{:S(2)}) async-start(), calls=%async_computation.3 | async-start | bytes 327680 | tf_op jit(solution)/shard_map/psum | solution.py:167
  147.6 49.2 %copy-start.5 = (f32[1280]{0:T(1024)S(1)}, f32[1280]{0:T(1024)}, u32[]{:S(2)}) copy-start(f32[1280]{0:T(1024)} %param.32) | copy-start | bytes 15364
  152.9 74.6 %reduce-scatter.5.cloned.1.call-start = ((), (), s32[]{:S(2)}) async-start(), calls=%async_computation.5 | async-start | bytes 1024000 | tf_op jit(solution)/shard_map/reduce_scatter | solution.py:180
  206.4 46.3 %reduce-scatter.3.cloned.1.call-start = ((), (), s32[]{:S(2)}) async-start(), calls=%async_computation.4 | async-start | bytes 1024000 | tf_op jit(solution)/shard_map/reduce_scatter | solution.py:179
  216.4 79.2 %all-reduce.10.cloned.1.call-start = ((), (), s32[]{:S(2)}) async-start(), calls=%async_computation.6 | async-start | bytes 327680 | tf_op jit(solution)/shard_map/psum | solution.py:186
  269.0 53.7 %copy-start.1 = (bf16[1280,256]{1,0:T(8,128)(2,1)S(1)}, bf16[1280,256]{1,0:T(8,128)(2,1)}, u32[]{:S(2)}) copy-start(bf16[1280,256]{1,0:T(8,128)(2,1)} %param.23) | copy-start | bytes 1966084
  278.3 42.8 %all-reduce.12.cloned.1.call-start = ((), (), s32[]{:S(2)}) async-start(), calls=%async_computation.7 | async-start | bytes 327680 | tf_op jit(solution)/shard_map/psum | solution.py:185
Sparse Core Ops, SparseCore 0:
  25.6 33.7 all-reduce.5
  75.0 50.2 all-gather.4
  153.0 31.0 all-reduce.7
  206.6 20.8 reduce-scatter.4
  229.6 22.9 reduce-scatter.2
  278.4 17.1 all-reduce.9
  297.9 23.1 all-reduce.11
